TPU v7x, 32 devices: a whole 2x2x4 slice. The times are simulated.
32 devices in a mesh: seq: 16 (over z, y, x), tp: 2 (over core).
Axes of the slice: x: 2, y: 2, z: 4, core: 2. Of those that a mesh axis runs over, the one named last changes fastest.
Arguments:
- tokens: bfloat16 [2048, 2048], P('seq'), may hold values from -6 to 6
- attn_gain: float32 [2048], replicated, may hold values from 0.1 to 1.9
- mlp_gain: float32 [2048], replicated, may hold values from 0.1 to 1.9
- w_query: float32 [2048, 2048], P('seq', 'tp'), may hold values from -0.70710678 to 0.70710678
- w_key: float32 [2048, 2048], P('seq', 'tp'), may hold values from -0.70710678 to 0.70710678
- w_value: float32 [2048, 2048], P('seq', 'tp'), may hold values from -0.125 to 0.125
- w_out: float32 [2048, 2048], P('tp', 'seq'), may hold values from -0.125 to 0.125
- sink_logits: float32 [16], P('tp'), may hold values from 8 to 16
- router: float32 [2048, 16], P('seq'), may hold values from -0.25 to 0.25
- expert_gate: float32 [16, 2048, 1024], P(None, 'seq', 'tp'), may hold values from -0.125 to 0.125
- expert_up: float32 [16, 2048, 1024], P(None, 'seq', 'tp'), may hold values from -0.125 to 0.125
- expert_down: float32 [16, 2048, 1024], P(None, 'seq', 'tp'), may hold values from -0.1875 to 0.1875
- layout_map: int32 [16], replicated, may hold values from 0 to 15, each once
- real_lengths: int32 [2], replicated, may hold values from 256 to 1088, as said below
- routes: int32 [2048, 8], P('seq'), may hold values from 0 to 15, all different within a row; in each aligned block of 128 rows (0 to 127, 128 to 255, ...) at most 72 rows name the same one
Outputs:
- layer_out: bfloat16 [2048, 2048], P('seq', 'tp')
Inputs may be any that keep to these rules, and one draw needn't show every extreme that they name: Prompt p has real tokens in the first real_lengths[p] of its slots and padding after them; each length is at least 256; the last prompt has no padding. `routes`: each row names 8 different experts; among the rows of one device no expert is named more than 72 times, and in some device some expert exactly 72 times. `layout_map`: each trainer expert is held by exactly one server expert number.
All inputs are finite; a program needn't handle non-finite values.
Results may differ from a plain program's by a relative error of at most 0.0075.
The roundings to bfloat16 on the way count: a program that leaves them out, or rounds other values in their place, can miss the bound.
Values may be sent and summed in bfloat16 or wider, within the bound.
No kernel may reach another device: no remote copies, remote signals or barrier semaphores. Data moves between devices by JAX's collectives and lax.ppermute only.
A program may use at most 128 MiB of HBM per device.

v0:
```python
import jax
import jax.numpy as jnp
from jax import lax
from jax.sharding import PartitionSpec as P

HEAD = 128
HALF_WIN = 2048
EPSILON = 1e-05
ROPE_BASE = 50000.0
MASKED = -1e30


def from_behind(value, axis, steps):
    count = lax.axis_size(axis)
    first, last = (max(0, -steps), min(count, count - steps))
    return lax.ppermute(value, axis, [(source, source + steps) for source in range(first, last)])


def rms_scale(row_values, gain_vector):
    mean_square = jnp.mean(row_values * row_values, axis=-1, keepdims=True)
    return row_values * lax.rsqrt(mean_square + EPSILON) * gain_vector


def rotate(head_block, positions):
    half_dim = head_block.shape[-1] // 2
    frequency = ROPE_BASE ** (-jnp.arange(half_dim, dtype=jnp.float32) / half_dim)
    angles = positions[:, None, None] * frequency[None, None, :]
    cosine = jnp.cos(angles)
    sine_part = jnp.sin(angles)
    first_half = head_block[..., :half_dim]
    second_half = head_block[..., half_dim:]
    return jnp.concatenate(
        [
            first_half * cosine - second_half * sine_part,
            second_half * cosine + first_half * sine_part,
        ],
        axis=-1,
    )


def length_of(prompt, real_lengths):
    one_hot = prompt[:, None] == jnp.arange(real_lengths.shape[0], dtype=jnp.int32)[None, :]
    return jnp.sum(jnp.where(one_hot, real_lengths[None, :], 0), axis=1)


def prompt_split(slot_ids, slot_len, stagger, prompt_count):
    prompt = jnp.minimum((slot_ids + stagger) // slot_len, prompt_count - 1)
    start = jnp.maximum(prompt * slot_len - stagger, 0)
    return (prompt, slot_ids - start)


def key_rules(query_ids, key_ids, slot_len, stagger, total_slots, real_lengths):
    prompt_count = real_lengths.shape[0]
    key_prompt, key_pos = prompt_split(key_ids, slot_len, stagger, prompt_count)
    query_prompt = prompt_split(query_ids, slot_len, stagger, prompt_count)[0]
    inside = (key_ids >= 0) & (key_ids < total_slots)
    key_live = inside & (key_pos < length_of(key_prompt, real_lengths))
    same_prompt = query_prompt[:, None] == key_prompt[None, :]
    nearby = jnp.abs(query_ids[:, None] - key_ids[None, :]) < HALF_WIN
    return same_prompt & nearby & key_live[None, :]


def attend(softmax_state, query_rows, key_rows, value_rows, allowed):
    running_max, denominator, accumulated = softmax_state
    scores = jnp.einsum(
        "tge,kge->gtk", query_rows, key_rows, preferred_element_type=jnp.float32
    ) * HEAD ** (-0.5)
    scores = jnp.where(allowed[None], scores, MASKED)
    new_max = jnp.maximum(running_max, jnp.max(scores, axis=2))
    rescale = jnp.exp(running_max - new_max)
    weight_tensors = jnp.exp(scores - new_max[:, :, None])
    denominator = denominator * rescale + jnp.sum(weight_tensors, axis=2)
    accumulated = accumulated * rescale[:, :, None] + jnp.einsum(
        "ytz,zyb->ytb",
        weight_tensors,
        value_rows.astype(jnp.float32),
        precision=lax.Precision.HIGHEST,
    )
    return (new_max, denominator, accumulated)


def shards(
    tokens,
    attn_gain,
    mlp_gain,
    w_query,
    w_key,
    w_value,
    w_out,
    sink_logits,
    router,
    expert_gate,
    expert_up,
    expert_down,
    layout_map,
    real_lengths,
    routes,
):
    token_count, model_width = tokens.shape
    seq_count = lax.axis_size("seq")
    tp_count = lax.axis_size("tp")
    expert_count = router.shape[1]
    route_count = routes.shape[1]
    head_count = sink_logits.shape[0]
    proj_width = head_count * HEAD
    col_share = model_width // tp_count
    total_slots = token_count * seq_count
    prompt_count = real_lengths.shape[0]
    slot_len = total_slots // prompt_count
    stagger = token_count // 2
    capacity = max(2, min(token_count, 9 * token_count * route_count // (8 * expert_count)))
    seq_place = lax.axis_index("seq")
    tp_place = lax.axis_index("tp")
    offsets = jnp.arange(token_count, dtype=jnp.int32)
    token_index = seq_place * token_count + offsets
    prompt, position = prompt_split(token_index, slot_len, stagger, prompt_count)
    valid_token = position < length_of(prompt, real_lengths)
    normed = rms_scale(tokens.astype(jnp.float32), attn_gain).astype(jnp.bfloat16)
    stack_local = jnp.concatenate([w_query, w_key, w_value], axis=1).astype(jnp.bfloat16)
    router_local = router.astype(jnp.bfloat16)
    stack_piece = lax.all_gather(stack_local, "seq", axis=0, tiled=True)
    router_piece = lax.all_gather(router_local, "seq", axis=0, tiled=True)
    product = jnp.dot(normed, stack_piece, preferred_element_type=jnp.float32)
    router_full = router_piece
    product, router_full = (product, router_full)
    rotary_positions = position.astype(jnp.float32)
    query_rows = rotate(
        product[:, :proj_width].reshape(token_count, head_count, HEAD), rotary_positions
    ).astype(jnp.bfloat16)
    key_rows = rotate(
        product[:, proj_width : 2 * proj_width].reshape(token_count, head_count, HEAD),
        rotary_positions,
    ).astype(jnp.bfloat16)
    value_rows = (
        product[:, 2 * proj_width :].astype(jnp.bfloat16).reshape(token_count, head_count, HEAD)
    )
    softmax_state = (
        jnp.broadcast_to(sink_logits[:, None], (head_count, token_count)),
        jnp.ones((head_count, token_count), jnp.float32),
        jnp.zeros((head_count, token_count, HEAD), jnp.float32),
    )
    softmax_state = attend(
        softmax_state,
        query_rows,
        key_rows,
        value_rows,
        key_rules(token_index, token_index, slot_len, stagger, total_slots, real_lengths),
    )
    own_pair = jnp.stack([key_rows, value_rows])

    def one_turn(turn_index, loop_carry):
        loop_state, from_below, from_above = loop_carry
        from_below = from_behind(from_below, "seq", 1)
        from_above = from_behind(from_above, "seq", -1)
        reach_rows = (turn_index + 1) * token_count
        key_ids = jnp.concatenate([token_index - reach_rows, token_index + reach_rows])
        neighbours = jnp.concatenate([from_below, from_above], axis=1)
        allowed = key_rules(token_index, key_ids, slot_len, stagger, total_slots, real_lengths)
        loop_state = attend(loop_state, query_rows, neighbours[0], neighbours[1], allowed)
        return (loop_state, from_below, from_above)

    softmax_state, from_below, from_above = lax.fori_loop(
        0, HALF_WIN // token_count, one_turn, (softmax_state, own_pair, own_pair)
    )
    running_max, denominator, accumulated = softmax_state
    attention_result = (
        jnp.transpose(accumulated / denominator[:, :, None], (1, 0, 2))
        .reshape(token_count, proj_width)
        .astype(jnp.bfloat16)
    )
    partial_out = jnp.dot(
        attention_result,
        lax.all_gather(w_out.astype(jnp.bfloat16), "seq", axis=1, tiled=True),
        preferred_element_type=jnp.float32,
    )
    mixed_full = lax.psum(partial_out, "tp")
    full_rows = tokens.astype(jnp.float32) + mixed_full
    outgoing = rms_scale(full_rows, mlp_gain).astype(jnp.bfloat16)
    logits = jnp.dot(outgoing, router_full, preferred_element_type=jnp.float32)
    residual = lax.dynamic_slice_in_dim(full_rows, tp_place * col_share, col_share, 1)
    expert_ids = jnp.arange(expert_count, dtype=jnp.int32)
    chosen = routes[:, :, None] == expert_ids[None, None, :]
    route_logits = jnp.sum(jnp.where(chosen, logits[:, None, :], 0.0), axis=2)
    route_weight = jax.nn.softmax(route_logits, axis=1) * valid_token[:, None]
    flat_routes = routes.reshape(-1)
    live_route = jnp.repeat(valid_token, route_count)
    one_hot = ((flat_routes[:, None] == expert_ids[None, :]) & live_route[:, None]).astype(
        jnp.int32
    )
    rank_within = jnp.sum((jnp.cumsum(one_hot, axis=0) - one_hot) * one_hot, axis=1)
    slot_index = flat_routes * capacity + rank_within
    target_slot = jnp.where(live_route, slot_index, expert_count * capacity)
    owner_row = jnp.repeat(offsets, route_count) + 1
    source_row = (
        jnp.zeros((expert_count * capacity,), jnp.int32).at[target_slot].set(owner_row, mode="drop")
    )
    buffer = jnp.where(
        (source_row > 0)[:, None],
        outgoing[jnp.maximum(source_row - 1, 0)],
        jnp.zeros((), jnp.bfloat16),
    )
    buffer = buffer.reshape(expert_count, capacity, outgoing.shape[1])
    trainer = jnp.concatenate([expert_gate, expert_up, expert_down], axis=2).astype(jnp.bfloat16)
    ordered = jnp.take(trainer, layout_map, axis=0)
    server = lax.all_to_all(ordered, "seq", split_axis=0, concat_axis=1, tiled=True)
    hidden_share = expert_gate.shape[2]
    local_experts = server.shape[0]
    full_block = lax.all_to_all(buffer, "seq", split_axis=0, concat_axis=0, tiled=True)
    item_count = full_block.shape[1]
    grouped = full_block.reshape(seq_count, local_experts, item_count, model_width)
    gate_up = jnp.einsum(
        "sacd,adf->sacf",
        grouped,
        server[:, :, : 2 * hidden_share],
        preferred_element_type=jnp.float32,
    )
    hidden_state = (jax.nn.silu(gate_up[..., :hidden_share]) * gate_up[..., hidden_share:]).astype(
        jnp.bfloat16
    )
    partial_rows = jnp.einsum(
        "sacf,adf->sacd",
        hidden_state,
        server[:, :, 2 * hidden_share :],
        preferred_element_type=jnp.float32,
    )
    partial_rows = lax.optimization_barrier(partial_rows.astype(jnp.bfloat16)).astype(jnp.float32)
    summed = lax.psum_scatter(
        partial_rows.astype(jnp.bfloat16), "tp", scatter_dimension=3, tiled=True
    )
    returned = lax.all_to_all(
        summed.reshape(seq_count * local_experts, item_count, col_share),
        "seq",
        split_axis=0,
        concat_axis=0,
        tiled=True,
    )
    picked = returned.reshape(expert_count * capacity, col_share)[
        jnp.where(live_route, slot_index, 0)
    ]
    picked = picked.reshape(token_count, route_count, col_share)
    expert_mix = jnp.sum(route_weight[:, :, None] * picked.astype(jnp.float32), axis=1)
    return (residual + expert_mix).astype(jnp.bfloat16)


def solution(mesh):
    placed = (
        P("seq", None),
        P(),
        P(),
        P("seq", "tp"),
        P("seq", "tp"),
        P("seq", "tp"),
        P("tp", "seq"),
        P("tp"),
        P("seq", None),
        P(None, "seq", "tp"),
        P(None, "seq", "tp"),
        P(None, "seq", "tp"),
        P(),
        P(),
        P("seq", None),
    )
    return jax.shard_map(
        shards, mesh=mesh, in_specs=placed, out_specs=P("seq", "tp"), check_vma=False
    )
```

profile of v0, /device:TPU:18, one launch (start us, length us, event | category | flops | bytes accessed | tf_op | source)
XLA Modules:
  0.0 1064.2 jit_solution(7470347210897196199)
XLA Ops:
  17.1 5.7 pad_maximum_fusion
  22.7 6.3 gather_fusion
  29.1 6.1 broadcast_select_fusion
  35.2 7.2 all-to-all-start
  50.4 233.6 %all-gather.3.cloned.1.call-done = bf16[2048,3072]{1,0:T(8,128)(2,1)} async-done(((bf16[128,3072]{1,0:T(8,128)(2,1)}), bf16[2048,3072]{1,0:T(8,128)(2,1)}) %all-gather.3.cloned.1.call-update) | async-done | bytes 12582928 | tf_op jit(solution)/shard_map/all_gather | solution.py:121
  283.9 6.5 fusion.21
  293.4 493.8 %while.25 = (s32[]{:T(128)}, f32[8,128]{1,0:T(8,128)S(1)}, f32[8,128]{1,0:T(8,128)S(1)}, f32[8,128,128]{2,1,0:T(8,128)S(1)}, bf16[2,128,8,128]{3,1,2,0:T(8,128)(...) while((s32[]{:T(128)}, f32[8,128]{1,0:T(8,128)S(1)}, ...), condition=%wide.region_8.9_spmd.clone, body=%wide.region_4.8_spmd.clone.sunk | while | flops 471806848 | bytes 14038749 | solution.py:162
  300.5 23.3 %collective-permute-done = bf16[2,128,8,128]{3,1,2,0:T(8,128)(2,1)S(1)} collective-permute-done((bf16[2,128,8,128]{3,1,2,0:T(8,128)(2,1)S(1)}, bf16[2,128,8,128]{3,1,2,0:T(8,128)(2,1)S(1)}, u32[]{:S(2)}, u32[]{:S(2)}) %collective-permute-start) | collective-permute-done | bytes 524320 | tf_op jit(solution)/shard_map/while/body/eval_jaxpr/ppermute | solution.py:16
  332.8 20.7 %collective-permute-done = bf16[2,128,8,128]{3,1,2,0:T(8,128)(2,1)S(1)} collective-permute-done((bf16[2,128,8,128]{3,1,2,0:T(8,128)(2,1)S(1)}, bf16[2,128,8,128]{3,1,2,0:T(8,128)(2,1)S(1)}, u32[]{:S(2)}, u32[]{:S(2)}) %collective-permute-start) | collective-permute-done | bytes 524320 | tf_op jit(solution)/shard_map/while/body/eval_jaxpr/ppermute | solution.py:16
  362.5 41.4 %collective-permute-done = bf16[2,128,8,128]{3,1,2,0:T(8,128)(2,1)S(1)} collective-permute-done((bf16[2,128,8,128]{3,1,2,0:T(8,128)(2,1)S(1)}, bf16[2,128,8,128]{3,1,2,0:T(8,128)(2,1)S(1)}, u32[]{:S(2)}, u32[]{:S(2)}) %collective-permute-start) | collective-permute-done | bytes 524320 | tf_op jit(solution)/shard_map/while/body/eval_jaxpr/ppermute | solution.py:16
  413.3 21.1 %collective-permute-done = bf16[2,128,8,128]{3,1,2,0:T(8,128)(2,1)S(1)} collective-permute-done((bf16[2,128,8,128]{3,1,2,0:T(8,128)(2,1)S(1)}, bf16[2,128,8,128]{3,1,2,0:T(8,128)(2,1)S(1)}, u32[]{:S(2)}, u32[]{:S(2)}) %collective-permute-start) | collective-permute-done | bytes 524320 | tf_op jit(solution)/shard_map/while/body/eval_jaxpr/ppermute | solution.py:16
  443.4 19.8 %collective-permute-done = bf16[2,128,8,128]{3,1,2,0:T(8,128)(2,1)S(1)} collective-permute-done((bf16[2,128,8,128]{3,1,2,0:T(8,128)(2,1)S(1)}, bf16[2,128,8,128]{3,1,2,0:T(8,128)(2,1)S(1)}, u32[]{:S(2)}, u32[]{:S(2)}) %collective-permute-start) | collective-permute-done | bytes 524320 | tf_op jit(solution)/shard_map/while/body/eval_jaxpr/ppermute | solution.py:16
  472.2 19.4 %collective-permute-done = bf16[2,128,8,128]{3,1,2,0:T(8,128)(2,1)S(1)} collective-permute-done((bf16[2,128,8,128]{3,1,2,0:T(8,128)(2,1)S(1)}, bf16[2,128,8,128]{3,1,2,0:T(8,128)(2,1)S(1)}, u32[]{:S(2)}, u32[]{:S(2)}) %collective-permute-start) | collective-permute-done | bytes 524320 | tf_op jit(solution)/shard_map/while/body/eval_jaxpr/ppermute | solution.py:16
  500.7 21.3 %collective-permute-done = bf16[2,128,8,128]{3,1,2,0:T(8,128)(2,1)S(1)} collective-permute-done((bf16[2,128,8,128]{3,1,2,0:T(8,128)(2,1)S(1)}, bf16[2,128,8,128]{3,1,2,0:T(8,128)(2,1)S(1)}, u32[]{:S(2)}, u32[]{:S(2)}) %collective-permute-start) | collective-permute-done | bytes 524320 | tf_op jit(solution)/shard_map/while/body/eval_jaxpr/ppermute | solution.py:16
  531.0 19.4 %collective-permute-done = bf16[2,128,8,128]{3,1,2,0:T(8,128)(2,1)S(1)} collective-permute-done((bf16[2,128,8,128]{3,1,2,0:T(8,128)(2,1)S(1)}, bf16[2,128,8,128]{3,1,2,0:T(8,128)(2,1)S(1)}, u32[]{:S(2)}, u32[]{:S(2)}) %collective-permute-start) | collective-permute-done | bytes 524320 | tf_op jit(solution)/shard_map/while/body/eval_jaxpr/ppermute | solution.py:16
  559.4 21.3 %collective-permute-done = bf16[2,128,8,128]{3,1,2,0:T(8,128)(2,1)S(1)} collective-permute-done((bf16[2,128,8,128]{3,1,2,0:T(8,128)(2,1)S(1)}, bf16[2,128,8,128]{3,1,2,0:T(8,128)(2,1)S(1)}, u32[]{:S(2)}, u32[]{:S(2)}) %collective-permute-start) | collective-permute-done | bytes 524320 | tf_op jit(solution)/shard_map/while/body/eval_jaxpr/ppermute | solution.py:16
  589.7 19.4 %collective-permute-done = bf16[2,128,8,128]{3,1,2,0:T(8,128)(2,1)S(1)} collective-permute-done((bf16[2,128,8,128]{3,1,2,0:T(8,128)(2,1)S(1)}, bf16[2,128,8,128]{3,1,2,0:T(8,128)(2,1)S(1)}, u32[]{:S(2)}, u32[]{:S(2)}) %collective-permute-start) | collective-permute-done | bytes 524320 | tf_op jit(solution)/shard_map/while/body/eval_jaxpr/ppermute | solution.py:16
  618.1 21.3 %collective-permute-done = bf16[2,128,8,128]{3,1,2,0:T(8,128)(2,1)S(1)} collective-permute-done((bf16[2,128,8,128]{3,1,2,0:T(8,128)(2,1)S(1)}, bf16[2,128,8,128]{3,1,2,0:T(8,128)(2,1)S(1)}, u32[]{:S(2)}, u32[]{:S(2)}) %collective-permute-start) | collective-permute-done | bytes 524320 | tf_op jit(solution)/shard_map/while/body/eval_jaxpr/ppermute | solution.py:16
  648.4 19.4 %collective-permute-done = bf16[2,128,8,128]{3,1,2,0:T(8,128)(2,1)S(1)} collective-permute-done((bf16[2,128,8,128]{3,1,2,0:T(8,128)(2,1)S(1)}, bf16[2,128,8,128]{3,1,2,0:T(8,128)(2,1)S(1)}, u32[]{:S(2)}, u32[]{:S(2)}) %collective-permute-start) | collective-permute-done | bytes 524320 | tf_op jit(solution)/shard_map/while/body/eval_jaxpr/ppermute | solution.py:16
  676.9 21.3 %collective-permute-done = bf16[2,128,8,128]{3,1,2,0:T(8,128)(2,1)S(1)} collective-permute-done((bf16[2,128,8,128]{3,1,2,0:T(8,128)(2,1)S(1)}, bf16[2,128,8,128]{3,1,2,0:T(8,128)(2,1)S(1)}, u32[]{:S(2)}, u32[]{:S(2)}) %collective-permute-start) | collective-permute-done | bytes 524320 | tf_op jit(solution)/shard_map/while/body/eval_jaxpr/ppermute | solution.py:16
  707.2 19.4 %collective-permute-done = bf16[2,128,8,128]{3,1,2,0:T(8,128)(2,1)S(1)} collective-permute-done((bf16[2,128,8,128]{3,1,2,0:T(8,128)(2,1)S(1)}, bf16[2,128,8,128]{3,1,2,0:T(8,128)(2,1)S(1)}, u32[]{:S(2)}, u32[]{:S(2)}) %collective-permute-start) | collective-permute-done | bytes 524320 | tf_op jit(solution)/shard_map/while/body/eval_jaxpr/ppermute | solution.py:16
  735.6 21.3 %collective-permute-done = bf16[2,128,8,128]{3,1,2,0:T(8,128)(2,1)S(1)} collective-permute-done((bf16[2,128,8,128]{3,1,2,0:T(8,128)(2,1)S(1)}, bf16[2,128,8,128]{3,1,2,0:T(8,128)(2,1)S(1)}, u32[]{:S(2)}, u32[]{:S(2)}) %collective-permute-start) | collective-permute-done | bytes 524320 | tf_op jit(solution)/shard_map/while/body/eval_jaxpr/ppermute | solution.py:16
  765.9 19.4 %collective-permute-done = bf16[2,128,8,128]{3,1,2,0:T(8,128)(2,1)S(1)} collective-permute-done((bf16[2,128,8,128]{3,1,2,0:T(8,128)(2,1)S(1)}, bf16[2,128,8,128]{3,1,2,0:T(8,128)(2,1)S(1)}, u32[]{:S(2)}, u32[]{:S(2)}) %collective-permute-start) | collective-permute-done | bytes 524320 | tf_op jit(solution)/shard_map/while/body/eval_jaxpr/ppermute | solution.py:16
  796.2 15.8 %all-reduce.2.cloned.1.call-done = f32[128,2048]{1,0:T(8,128)} async-done(((f32[128,2048]{1,0:T(8,128)}), f32[128,2048]{1,0:T(8,128)}) %all-reduce.2.cloned.1.call-update) | async-done | bytes 1048592 | tf_op jit(solution)/shard_map/psum | solution.py:176
  814.6 6.0 gather_fusion.1
  825.4 110.3 %all_to_all.22 = bf16[16,72,2048]{2,1,0:T(8,128)(2,1)S(1)} all-to-all(bf16[16,72,2048]{2,1,0:T(8,128)(2,1)} %broadcast_select_fusion.1), channel_id=1, replica_groups=mesh['seq'=16,'tp'=2] {'seq'}, dimensions={0} | all-to-all | bytes 9437184 | tf_op jit(solution)/shard_map/all_to_all | solution.py:208
  935.7 7.3 fusion.14
  943.0 5.9 convert_bitcast_fusion
  949.0 13.0 %reduce-scatter.2.cloned.1.call-done = bf16[16,1,72,1024]{3,2,0,1:T(8,128)(2,1)} async-done(((bf16[16,1,72,2048]{3,2,0,1:T(8,128)(2,1)}), bf16[16,1,72,1024]{3,2,0,1:T(8,128)(2,1)}) %reduce-scatter.2.cloned.1.call-update) | async-done | bytes 2359312 | tf_op jit(solution)/shard_map/reduce_scatter | solution.py:227
  962.0 7.0 all-to-all-start.2
  968.9 78.2 %all_gather.11 = bf16[2048,16]{0,1:T(8,128)(2,1)S(1)} all-gather(bf16[128,16]{0,1:T(8,128)(2,1)S(1)} %convert_element_type.94), channel_id=1, replica_groups=mesh['seq'=16,'tp'=2] {'seq'}, dimensions={0}, use_global_device_ids=true | all-gather | bytes 69632 | tf_op jit(solution)/shard_map/all_gather | solution.py:122
  1047.5 5.4 gather_fusion.2
  (423 shorter events, 184.9 us)
Async XLA Ops:
  6.5 277.4 %all-gather.3.cloned.1.call-start = ((), (), s32[]{:S(2)}) async-start(), calls=%async_computation.4 | async-start | bytes 13369344 | tf_op jit(solution)/shard_map/all_gather | solution.py:121
  35.2 790.3 %all-to-all-start = ((bf16[16,128,1536]{2,1,0:T(8,128)(2,1)}), bf16[16,128,1536]{2,1,0:T(8,128)(2,1)}, u32[]{:S(2)}, u32[]{:S(2)}) async-start(bf16[16,128,1536]{2,1,0:T(8,128)(2,1)} %broadcast_select_fusion), calls=%async_computation | async-start | bytes 12582912 | tf_op jit(solution)/shard_map/all_to_all | solution.py:205
  42.4 745.1 %all-gather.5.cloned.1.call-start = ((), (), s32[]{:S(2)}) async-start(), calls=%async_computation.5 | async-start | bytes 4456448 | tf_op jit(solution)/shard_map/all_gather | solution.py:173
  43.2 768.7 %all-reduce.2.cloned.1.call-start = ((), (), s32[]{:S(2)}) async-start(), calls=%async_computation.6 | async-start | bytes 2097152 | tf_op jit(solution)/shard_map/psum | solution.py:176
  293.4 30.4 %collective-permute-start.1 = (bf16[2,128,8,128]{3,1,2,0:T(8,128)(2,1)S(1)}, bf16[2,128,8,128]{3,1,2,0:T(8,128)(2,1)S(1)}, u32[]{:S(2)}, u32[]{:S(2)}) collective-permute-start(bf16[2,128,8,128]{3,1,2,0:T(8,128)(2,1)S(1)} %get-tuple-element.428), channel_id=1, source_target_pairs={{2,0},{4,2},{6,4},{8,6},{10,8},{12,10},{14,12},{16,14},{18,16},{20... | collective-permute-start | bytes 1572872 | tf_op jit(solution)/shard_map/while/body/eval_jaxpr/ppermute | solution.py:16
  296.1 27.7 %collective-permute-start = (bf16[2,128,8,128]{3,1,2,0:T(8,128)(2,1)S(1)}, bf16[2,128,8,128]{3,1,2,0:T(8,128)(2,1)S(1)}, u32[]{:S(2)}, u32[]{:S(2)}) collective-permute-start(bf16[2,128,8,128]{3,1,2,0:T(8,128)(2,1)S(1)} %get-tuple-element.427), channel_id=1, source_target_pairs={{0,2},{2,4},{4,6},{6,8},{8,10},{10,12},{12,14},{14,16},{16,18},{18... | collective-permute-start | bytes 1572872 | tf_op jit(solution)/shard_map/while/body/eval_jaxpr/ppermute | solution.py:16
  325.7 27.8 %collective-permute-start.1 = (bf16[2,128,8,128]{3,1,2,0:T(8,128)(2,1)S(1)}, bf16[2,128,8,128]{3,1,2,0:T(8,128)(2,1)S(1)}, u32[]{:S(2)}, u32[]{:S(2)}) collective-permute-start(bf16[2,128,8,128]{3,1,2,0:T(8,128)(2,1)S(1)} %get-tuple-element.428), channel_id=1, source_target_pairs={{2,0},{4,2},{6,4},{8,6},{10,8},{12,10},{14,12},{16,14},{18,16},{20... | collective-permute-start | bytes 1572872 | tf_op jit(solution)/shard_map/while/body/eval_jaxpr/ppermute | solution.py:16
  327.6 25.8 %collective-permute-start = (bf16[2,128,8,128]{3,1,2,0:T(8,128)(2,1)S(1)}, bf16[2,128,8,128]{3,1,2,0:T(8,128)(2,1)S(1)}, u32[]{:S(2)}, u32[]{:S(2)}) collective-permute-start(bf16[2,128,8,128]{3,1,2,0:T(8,128)(2,1)S(1)} %get-tuple-element.427), channel_id=1, source_target_pairs={{0,2},{2,4},{4,6},{6,8},{8,10},{10,12},{12,14},{14,16},{16,18},{18... | collective-permute-start | bytes 1572872 | tf_op jit(solution)/shard_map/while/body/eval_jaxpr/ppermute | solution.py:16
  355.4 48.5 %collective-permute-start.1 = (bf16[2,128,8,128]{3,1,2,0:T(8,128)(2,1)S(1)}, bf16[2,128,8,128]{3,1,2,0:T(8,128)(2,1)S(1)}, u32[]{:S(2)}, u32[]{:S(2)}) collective-permute-start(bf16[2,128,8,128]{3,1,2,0:T(8,128)(2,1)S(1)} %get-tuple-element.428), channel_id=1, source_target_pairs={{2,0},{4,2},{6,4},{8,6},{10,8},{12,10},{14,12},{16,14},{18,16},{20... | collective-permute-start | bytes 1572872 | tf_op jit(solution)/shard_map/while/body/eval_jaxpr/ppermute | solution.py:16
  359.3 44.6 %collective-permute-start = (bf16[2,128,8,128]{3,1,2,0:T(8,128)(2,1)S(1)}, bf16[2,128,8,128]{3,1,2,0:T(8,128)(2,1)S(1)}, u32[]{:S(2)}, u32[]{:S(2)}) collective-permute-start(bf16[2,128,8,128]{3,1,2,0:T(8,128)(2,1)S(1)} %get-tuple-element.427), channel_id=1, source_target_pairs={{0,2},{2,4},{4,6},{6,8},{8,10},{10,12},{12,14},{14,16},{16,18},{18... | collective-permute-start | bytes 1572872 | tf_op jit(solution)/shard_map/while/body/eval_jaxpr/ppermute | solution.py:16
  405.8 28.7 %collective-permute-start.1 = (bf16[2,128,8,128]{3,1,2,0:T(8,128)(2,1)S(1)}, bf16[2,128,8,128]{3,1,2,0:T(8,128)(2,1)S(1)}, u32[]{:S(2)}, u32[]{:S(2)}) collective-permute-start(bf16[2,128,8,128]{3,1,2,0:T(8,128)(2,1)S(1)} %get-tuple-element.428), channel_id=1, source_target_pairs={{2,0},{4,2},{6,4},{8,6},{10,8},{12,10},{14,12},{16,14},{18,16},{20... | collective-permute-start | bytes 1572872 | tf_op jit(solution)/shard_map/while/body/eval_jaxpr/ppermute | solution.py:16
  407.7 26.7 %collective-permute-start = (bf16[2,128,8,128]{3,1,2,0:T(8,128)(2,1)S(1)}, bf16[2,128,8,128]{3,1,2,0:T(8,128)(2,1)S(1)}, u32[]{:S(2)}, u32[]{:S(2)}) collective-permute-start(bf16[2,128,8,128]{3,1,2,0:T(8,128)(2,1)S(1)} %get-tuple-element.427), channel_id=1, source_target_pairs={{0,2},{2,4},{4,6},{6,8},{8,10},{10,12},{12,14},{14,16},{16,18},{18... | collective-permute-start | bytes 1572872 | tf_op jit(solution)/shard_map/while/body/eval_jaxpr/ppermute | solution.py:16
  436.3 27.0 %collective-permute-start.1 = (bf16[2,128,8,128]{3,1,2,0:T(8,128)(2,1)S(1)}, bf16[2,128,8,128]{3,1,2,0:T(8,128)(2,1)S(1)}, u32[]{:S(2)}, u32[]{:S(2)}) collective-permute-start(bf16[2,128,8,128]{3,1,2,0:T(8,128)(2,1)S(1)} %get-tuple-element.428), channel_id=1, source_target_pairs={{2,0},{4,2},{6,4},{8,6},{10,8},{12,10},{14,12},{16,14},{18,16},{20... | collective-permute-start | bytes 1572872 | tf_op jit(solution)/shard_map/while/body/eval_jaxpr/ppermute | solution.py:16
  438.2 25.0 %collective-permute-start = (bf16[2,128,8,128]{3,1,2,0:T(8,128)(2,1)S(1)}, bf16[2,128,8,128]{3,1,2,0:T(8,128)(2,1)S(1)}, u32[]{:S(2)}, u32[]{:S(2)}) collective-permute-start(bf16[2,128,8,128]{3,1,2,0:T(8,128)(2,1)S(1)} %get-tuple-element.427), channel_id=1, source_target_pairs={{0,2},{2,4},{4,6},{6,8},{8,10},{10,12},{12,14},{14,16},{16,18},{18... | collective-permute-start | bytes 1572872 | tf_op jit(solution)/shard_map/while/body/eval_jaxpr/ppermute | solution.py:16
  465.1 26.6 %collective-permute-start.1 = (bf16[2,128,8,128]{3,1,2,0:T(8,128)(2,1)S(1)}, bf16[2,128,8,128]{3,1,2,0:T(8,128)(2,1)S(1)}, u32[]{:S(2)}, u32[]{:S(2)}) collective-permute-start(bf16[2,128,8,128]{3,1,2,0:T(8,128)(2,1)S(1)} %get-tuple-element.428), channel_id=1, source_target_pairs={{2,0},{4,2},{6,4},{8,6},{10,8},{12,10},{14,12},{16,14},{18,16},{20... | collective-permute-start | bytes 1572872 | tf_op jit(solution)/shard_map/while/body/eval_jaxpr/ppermute | solution.py:16
  493.6 28.4 %collective-permute-start.1 = (bf16[2,128,8,128]{3,1,2,0:T(8,128)(2,1)S(1)}, bf16[2,128,8,128]{3,1,2,0:T(8,128)(2,1)S(1)}, u32[]{:S(2)}, u32[]{:S(2)}) collective-permute-start(bf16[2,128,8,128]{3,1,2,0:T(8,128)(2,1)S(1)} %get-tuple-element.428), channel_id=1, source_target_pairs={{2,0},{4,2},{6,4},{8,6},{10,8},{12,10},{14,12},{16,14},{18,16},{20... | collective-permute-start | bytes 1572872 | tf_op jit(solution)/shard_map/while/body/eval_jaxpr/ppermute | solution.py:16
  495.5 26.5 %collective-permute-start = (bf16[2,128,8,128]{3,1,2,0:T(8,128)(2,1)S(1)}, bf16[2,128,8,128]{3,1,2,0:T(8,128)(2,1)S(1)}, u32[]{:S(2)}, u32[]{:S(2)}) collective-permute-start(bf16[2,128,8,128]{3,1,2,0:T(8,128)(2,1)S(1)} %get-tuple-element.427), channel_id=1, source_target_pairs={{0,2},{2,4},{4,6},{6,8},{8,10},{10,12},{12,14},{14,16},{16,18},{18... | collective-permute-start | bytes 1572872 | tf_op jit(solution)/shard_map/while/body/eval_jaxpr/ppermute | solution.py:16
  523.9 26.6 %collective-permute-start.1 = (bf16[2,128,8,128]{3,1,2,0:T(8,128)(2,1)S(1)}, bf16[2,128,8,128]{3,1,2,0:T(8,128)(2,1)S(1)}, u32[]{:S(2)}, u32[]{:S(2)}) collective-permute-start(bf16[2,128,8,128]{3,1,2,0:T(8,128)(2,1)S(1)} %get-tuple-element.428), channel_id=1, source_target_pairs={{2,0},{4,2},{6,4},{8,6},{10,8},{12,10},{14,12},{16,14},{18,16},{20... | collective-permute-start | bytes 1572872 | tf_op jit(solution)/shard_map/while/body/eval_jaxpr/ppermute | solution.py:16
  552.3 28.4 %collective-permute-start.1 = (bf16[2,128,8,128]{3,1,2,0:T(8,128)(2,1)S(1)}, bf16[2,128,8,128]{3,1,2,0:T(8,128)(2,1)S(1)}, u32[]{:S(2)}, u32[]{:S(2)}) collective-permute-start(bf16[2,128,8,128]{3,1,2,0:T(8,128)(2,1)S(1)} %get-tuple-element.428), channel_id=1, source_target_pairs={{2,0},{4,2},{6,4},{8,6},{10,8},{12,10},{14,12},{16,14},{18,16},{20... | collective-permute-start | bytes 1572872 | tf_op jit(solution)/shard_map/while/body/eval_jaxpr/ppermute | solution.py:16
  554.2 26.5 %collective-permute-start = (bf16[2,128,8,128]{3,1,2,0:T(8,128)(2,1)S(1)}, bf16[2,128,8,128]{3,1,2,0:T(8,128)(2,1)S(1)}, u32[]{:S(2)}, u32[]{:S(2)}) collective-permute-start(bf16[2,128,8,128]{3,1,2,0:T(8,128)(2,1)S(1)} %get-tuple-element.427), channel_id=1, source_target_pairs={{0,2},{2,4},{4,6},{6,8},{8,10},{10,12},{12,14},{14,16},{16,18},{18... | collective-permute-start | bytes 1572872 | tf_op jit(solution)/shard_map/while/body/eval_jaxpr/ppermute | solution.py:16
  582.6 26.6 %collective-permute-start.1 = (bf16[2,128,8,128]{3,1,2,0:T(8,128)(2,1)S(1)}, bf16[2,128,8,128]{3,1,2,0:T(8,128)(2,1)S(1)}, u32[]{:S(2)}, u32[]{:S(2)}) collective-permute-start(bf16[2,128,8,128]{3,1,2,0:T(8,128)(2,1)S(1)} %get-tuple-element.428), channel_id=1, source_target_pairs={{2,0},{4,2},{6,4},{8,6},{10,8},{12,10},{14,12},{16,14},{18,16},{20... | collective-permute-start | bytes 1572872 | tf_op jit(solution)/shard_map/while/body/eval_jaxpr/ppermute | solution.py:16
  611.0 28.4 %collective-permute-start.1 = (bf16[2,128,8,128]{3,1,2,0:T(8,128)(2,1)S(1)}, bf16[2,128,8,128]{3,1,2,0:T(8,128)(2,1)S(1)}, u32[]{:S(2)}, u32[]{:S(2)}) collective-permute-start(bf16[2,128,8,128]{3,1,2,0:T(8,128)(2,1)S(1)} %get-tuple-element.428), channel_id=1, source_target_pairs={{2,0},{4,2},{6,4},{8,6},{10,8},{12,10},{14,12},{16,14},{18,16},{20... | collective-permute-start | bytes 1572872 | tf_op jit(solution)/shard_map/while/body/eval_jaxpr/ppermute | solution.py:16
  613.0 26.5 %collective-permute-start = (bf16[2,128,8,128]{3,1,2,0:T(8,128)(2,1)S(1)}, bf16[2,128,8,128]{3,1,2,0:T(8,128)(2,1)S(1)}, u32[]{:S(2)}, u32[]{:S(2)}) collective-permute-start(bf16[2,128,8,128]{3,1,2,0:T(8,128)(2,1)S(1)} %get-tuple-element.427), channel_id=1, source_target_pairs={{0,2},{2,4},{4,6},{6,8},{8,10},{10,12},{12,14},{14,16},{16,18},{18... | collective-permute-start | bytes 1572872 | tf_op jit(solution)/shard_map/while/body/eval_jaxpr/ppermute | solution.py:16
  641.3 26.6 %collective-permute-start.1 = (bf16[2,128,8,128]{3,1,2,0:T(8,128)(2,1)S(1)}, bf16[2,128,8,128]{3,1,2,0:T(8,128)(2,1)S(1)}, u32[]{:S(2)}, u32[]{:S(2)}) collective-permute-start(bf16[2,128,8,128]{3,1,2,0:T(8,128)(2,1)S(1)} %get-tuple-element.428), channel_id=1, source_target_pairs={{2,0},{4,2},{6,4},{8,6},{10,8},{12,10},{14,12},{16,14},{18,16},{20... | collective-permute-start | bytes 1572872 | tf_op jit(solution)/shard_map/while/body/eval_jaxpr/ppermute | solution.py:16
  669.8 28.4 %collective-permute-start.1 = (bf16[2,128,8,128]{3,1,2,0:T(8,128)(2,1)S(1)}, bf16[2,128,8,128]{3,1,2,0:T(8,128)(2,1)S(1)}, u32[]{:S(2)}, u32[]{:S(2)}) collective-permute-start(bf16[2,128,8,128]{3,1,2,0:T(8,128)(2,1)S(1)} %get-tuple-element.428), channel_id=1, source_target_pairs={{2,0},{4,2},{6,4},{8,6},{10,8},{12,10},{14,12},{16,14},{18,16},{20... | collective-permute-start | bytes 1572872 | tf_op jit(solution)/shard_map/while/body/eval_jaxpr/ppermute | solution.py:16
  671.7 26.5 %collective-permute-start = (bf16[2,128,8,128]{3,1,2,0:T(8,128)(2,1)S(1)}, bf16[2,128,8,128]{3,1,2,0:T(8,128)(2,1)S(1)}, u32[]{:S(2)}, u32[]{:S(2)}) collective-permute-start(bf16[2,128,8,128]{3,1,2,0:T(8,128)(2,1)S(1)} %get-tuple-element.427), channel_id=1, source_target_pairs={{0,2},{2,4},{4,6},{6,8},{8,10},{10,12},{12,14},{14,16},{16,18},{18... | collective-permute-start | bytes 1572872 | tf_op jit(solution)/shard_map/while/body/eval_jaxpr/ppermute | solution.py:16
  700.1 26.6 %collective-permute-start.1 = (bf16[2,128,8,128]{3,1,2,0:T(8,128)(2,1)S(1)}, bf16[2,128,8,128]{3,1,2,0:T(8,128)(2,1)S(1)}, u32[]{:S(2)}, u32[]{:S(2)}) collective-permute-start(bf16[2,128,8,128]{3,1,2,0:T(8,128)(2,1)S(1)} %get-tuple-element.428), channel_id=1, source_target_pairs={{2,0},{4,2},{6,4},{8,6},{10,8},{12,10},{14,12},{16,14},{18,16},{20... | collective-permute-start | bytes 1572872 | tf_op jit(solution)/shard_map/while/body/eval_jaxpr/ppermute | solution.py:16
  728.5 28.4 %collective-permute-start.1 = (bf16[2,128,8,128]{3,1,2,0:T(8,128)(2,1)S(1)}, bf16[2,128,8,128]{3,1,2,0:T(8,128)(2,1)S(1)}, u32[]{:S(2)}, u32[]{:S(2)}) collective-permute-start(bf16[2,128,8,128]{3,1,2,0:T(8,128)(2,1)S(1)} %get-tuple-element.428), channel_id=1, source_target_pairs={{2,0},{4,2},{6,4},{8,6},{10,8},{12,10},{14,12},{16,14},{18,16},{20... | collective-permute-start | bytes 1572872 | tf_op jit(solution)/shard_map/while/body/eval_jaxpr/ppermute | solution.py:16
  730.4 26.5 %collective-permute-start = (bf16[2,128,8,128]{3,1,2,0:T(8,128)(2,1)S(1)}, bf16[2,128,8,128]{3,1,2,0:T(8,128)(2,1)S(1)}, u32[]{:S(2)}, u32[]{:S(2)}) collective-permute-start(bf16[2,128,8,128]{3,1,2,0:T(8,128)(2,1)S(1)} %get-tuple-element.427), channel_id=1, source_target_pairs={{0,2},{2,4},{4,6},{6,8},{8,10},{10,12},{12,14},{14,16},{16,18},{18... | collective-permute-start | bytes 1572872 | tf_op jit(solution)/shard_map/while/body/eval_jaxpr/ppermute | solution.py:16
  758.8 26.6 %collective-permute-start.1 = (bf16[2,128,8,128]{3,1,2,0:T(8,128)(2,1)S(1)}, bf16[2,128,8,128]{3,1,2,0:T(8,128)(2,1)S(1)}, u32[]{:S(2)}, u32[]{:S(2)}) collective-permute-start(bf16[2,128,8,128]{3,1,2,0:T(8,128)(2,1)S(1)} %get-tuple-element.428), channel_id=1, source_target_pairs={{2,0},{4,2},{6,4},{8,6},{10,8},{12,10},{14,12},{16,14},{18,16},{20... | collective-permute-start | bytes 1572872 | tf_op jit(solution)/shard_map/while/body/eval_jaxpr/ppermute | solution.py:16
  791.5 170.5 %reduce-scatter.2.cloned.1.call-start = ((), (), s32[]{:S(2)}) async-start(), calls=%async_computation.7 | async-start | bytes 7077888 | tf_op jit(solution)/shard_map/reduce_scatter | solution.py:227
  962.0 85.6 %all-to-all-start.2 = ((bf16[16,72,1024]{2,1,0:T(8,128)(2,1)}), bf16[16,72,1024]{2,1,0:T(8,128)(2,1)S(1)}, u32[]{:S(2)}, u32[]{:S(2)}) async-start(bf16[16,72,1024]{2,1,0:T(8,128)(2,1)} %bitcast.102), calls=%async_computation.3 | async-start | bytes 4718592 | tf_op jit(solution)/shard_map/all_to_all | solution.py:230
  (18 other events, 485.5 us)
Sparse Core Ops, SparseCore 0:
  10.9 272.9 all-gather.2
  286.6 137.9 all-gather.4
  791.6 20.3 all-reduce.1
  949.1 12.8 reduce-scatter.1
where the time goes:
time: 1070 us; the launch traced here: 1060 us
  waiting for transfers between devices  612 us (57%)
  blocking collectives  188 us (18%)
  starting transfers between devices  123 us (11%)
  matrix products  48.1 us (4%)
  other arithmetic  45.3 us (4%)
  local copies, waits for them, and re-layouts  31.9 us (3%)
  between operations  13.6 us (1%)
    ppermute x32, waiting for transfers between devices, from_behind(): lax.ppermute(value, axis, [(source, source + steps) for source in range(f...  349 us
    all_gather x1, waiting for transfers between devices, shards(): stack_piece = lax.all_gather(stack_local, 'seq', axis=0, tiled=True)  234 us
    all_to_all x1, blocking collectives, shards(): lax.all_to_all(buffer, 'seq', split_axis=0, concat_axis=0, tiled=True)  110 us
    ppermute x32, starting transfers between devices, from_behind(): lax.ppermute(value, axis, [(source, source + steps) for source in range(f...  108 us
    all_gather x1, blocking collectives, shards(): router_piece = lax.all_gather(router_local, 'seq', axis=0, tiled=True)  78.2 us
  transfers between devices with their start and end apart: 38, of which 19 were waited for; matrix products, arithmetic and copies ran while one was open for 9% of the time, Pallas kernels for 0%

commit v1 on v0

--- a/solution.py
+++ b/solution.py
@@ -119,7 +119,14 @@
     stack_local = jnp.concatenate([w_query, w_key, w_value], axis=1).astype(jnp.bfloat16)
     router_local = router.astype(jnp.bfloat16)
     stack_piece = lax.all_gather(stack_local, "seq", axis=0, tiled=True)
-    router_piece = lax.all_gather(router_local, "seq", axis=0, tiled=True)
+    size = lax.axis_size("seq")
+    right = [(i, (i + 1) % size) for i in range(size)]
+    shards_2 = [router_local]
+    for hop in range(1, size):
+        shards_2 = [lax.ppermute(shards_2[0], "seq", right), *shards_2]
+    full = jnp.concatenate(shards_2, axis=0)
+    shift = (lax.axis_index("seq") + 1) * shards_2[-1].shape[0]
+    router_piece = jnp.roll(full, shift, axis=0)
     product = jnp.dot(normed, stack_piece, preferred_element_type=jnp.float32)
     router_full = router_piece
     product, router_full = (product, router_full)

time: 1070 us -> 1110 us (1.037)
  waiting for transfers between devices: 612 us -> 695 us
  blocking collectives: 188 us -> 110 us
  starting transfers between devices: 123 us -> 164 us
    all_gather x1 -> x0, blocking collectives: 78.2 us -> none  [shards(): router_piece = lax.all_gather(router_local, 'seq', axis=0, tiled=True)]
    ppermute x0 -> x15, waiting for transfers between devices: none -> 63.3 us  [shards(): shards_2 = [lax.ppermute(shards_2[0], 'seq', right), *shards_2]]
    all_to_all x1, waiting for transfers between devices: 0.01 us -> 32.9 us  [shards(): lax.all_to_all(summed.reshape(seq_count * local_experts, item_count, col_...]
    all_to_all x1, starting transfers between devices: 6.97 us -> 34.7 us  [shards(): lax.all_to_all(summed.reshape(seq_count * local_experts, item_count, col_...]
    ppermute x0 -> x15, starting transfers between devices: none -> 13.1 us  [shards(): shards_2 = [lax.ppermute(shards_2[0], 'seq', right), *shards_2]]
    reduce_scatter x1, waiting for transfers between devices: 13 us -> 0.01 us  [shards(): lax.psum_scatter(partial_rows.astype(jnp.bfloat16), 'tp', scatter_dimensi...]
  transfers between devices with their start and end apart: 38 -> 53, of which waited for: 19 -> 33; matrix products, arithmetic and copies ran while one was open for 9% -> 8% of each run, Pallas kernels for 0% -> 0%
where the time goes in v1:
time: 1110 us
  waiting for transfers between devices  695 us (63%)
  starting transfers between devices  164 us (15%)
  blocking collectives  110 us (10%)
  matrix products  48.1 us (4%)
  other arithmetic  45.3 us (4%)
  local copies, waits for them, and re-layouts  32.8 us (3%)
  between operations  13.7 us (1%)
    ppermute x32, waiting for transfers between devices, from_behind(): lax.ppermute(value, axis, [(source, source + steps) for source in range(f...  349 us
    all_gather x1, waiting for transfers between devices, shards(): stack_piece = lax.all_gather(stack_local, 'seq', axis=0, tiled=True)  234 us
    all_to_all x1, blocking collectives, shards(): lax.all_to_all(buffer, 'seq', split_axis=0, concat_axis=0, tiled=True)  110 us
    ppermute x32, starting transfers between devices, from_behind(): lax.ppermute(value, axis, [(source, source + steps) for source in range(f...  108 us
    ppermute x15, waiting for transfers between devices, shards(): shards_2 = [lax.ppermute(shards_2[0], 'seq', right), *shards_2]  63.3 us
    all_to_all x1, starting transfers between devices, shards(): lax.all_to_all(summed.reshape(seq_count * local_experts, item_count, col_...  34.7 us
    all_to_all x1, waiting for transfers between devices, shards(): lax.all_to_all(summed.reshape(seq_count * local_experts, item_count, col_...  32.9 us
  transfers between devices with their start and end apart: 53, of which 33 were waited for; matrix products, arithmetic and copies ran while one was open for 8% of the time, Pallas kernels for 0%

profile of v1, /device:TPU:18, one launch (start us, length us, event | category | flops | bytes accessed | tf_op | source)
XLA Modules:
  0.0 1111.2 jit_solution(5125734608248558720)
XLA Ops:
  17.1 5.7 pad_maximum_fusion
  22.8 6.3 gather_fusion
  29.1 6.1 broadcast_select_fusion
  35.2 7.2 all-to-all-start
  50.4 233.6 %all-gather.3.cloned.1.call-done = bf16[2048,3072]{1,0:T(8,128)(2,1)} async-done(((bf16[128,3072]{1,0:T(8,128)(2,1)}), bf16[2048,3072]{1,0:T(8,128)(2,1)}) %all-gather.3.cloned.1.call-update) | async-done | bytes 12582928 | tf_op jit(solution)/shard_map/all_gather | solution.py:121
  284.0 6.5 fusion.21
  293.5 493.9 %while.25 = (s32[]{:T(128)}, f32[8,128]{1,0:T(8,128)S(1)}, f32[8,128]{1,0:T(8,128)S(1)}, f32[8,128,128]{2,1,0:T(8,128)S(1)}, bf16[2,128,8,128]{3,1,2,0:T(8,128)(...) while((s32[]{:T(128)}, f32[8,128]{1,0:T(8,128)S(1)}, ...), condition=%wide.region_8.9_spmd.clone, body=%wide.region_4.8_spmd.clone.sunk | while | flops 471806848 | bytes 14038749 | solution.py:169
  300.6 23.3 %collective-permute-done = bf16[2,128,8,128]{3,1,2,0:T(8,128)(2,1)S(1)} collective-permute-done((bf16[2,128,8,128]{3,1,2,0:T(8,128)(2,1)S(1)}, bf16[2,128,8,128]{3,1,2,0:T(8,128)(2,1)S(1)}, u32[]{:S(2)}, u32[]{:S(2)}) %collective-permute-start) | collective-permute-done | bytes 524320 | tf_op jit(solution)/shard_map/while/body/eval_jaxpr/ppermute | solution.py:16
  332.9 20.7 %collective-permute-done = bf16[2,128,8,128]{3,1,2,0:T(8,128)(2,1)S(1)} collective-permute-done((bf16[2,128,8,128]{3,1,2,0:T(8,128)(2,1)S(1)}, bf16[2,128,8,128]{3,1,2,0:T(8,128)(2,1)S(1)}, u32[]{:S(2)}, u32[]{:S(2)}) %collective-permute-start) | collective-permute-done | bytes 524320 | tf_op jit(solution)/shard_map/while/body/eval_jaxpr/ppermute | solution.py:16
  362.6 41.3 %collective-permute-done = bf16[2,128,8,128]{3,1,2,0:T(8,128)(2,1)S(1)} collective-permute-done((bf16[2,128,8,128]{3,1,2,0:T(8,128)(2,1)S(1)}, bf16[2,128,8,128]{3,1,2,0:T(8,128)(2,1)S(1)}, u32[]{:S(2)}, u32[]{:S(2)}) %collective-permute-start) | collective-permute-done | bytes 524320 | tf_op jit(solution)/shard_map/while/body/eval_jaxpr/ppermute | solution.py:16
  413.4 21.1 %collective-permute-done = bf16[2,128,8,128]{3,1,2,0:T(8,128)(2,1)S(1)} collective-permute-done((bf16[2,128,8,128]{3,1,2,0:T(8,128)(2,1)S(1)}, bf16[2,128,8,128]{3,1,2,0:T(8,128)(2,1)S(1)}, u32[]{:S(2)}, u32[]{:S(2)}) %collective-permute-start) | collective-permute-done | bytes 524320 | tf_op jit(solution)/shard_map/while/body/eval_jaxpr/ppermute | solution.py:16
  443.5 19.7 %collective-permute-done = bf16[2,128,8,128]{3,1,2,0:T(8,128)(2,1)S(1)} collective-permute-done((bf16[2,128,8,128]{3,1,2,0:T(8,128)(2,1)S(1)}, bf16[2,128,8,128]{3,1,2,0:T(8,128)(2,1)S(1)}, u32[]{:S(2)}, u32[]{:S(2)}) %collective-permute-start) | collective-permute-done | bytes 524320 | tf_op jit(solution)/shard_map/while/body/eval_jaxpr/ppermute | solution.py:16
  472.3 19.5 %collective-permute-done = bf16[2,128,8,128]{3,1,2,0:T(8,128)(2,1)S(1)} collective-permute-done((bf16[2,128,8,128]{3,1,2,0:T(8,128)(2,1)S(1)}, bf16[2,128,8,128]{3,1,2,0:T(8,128)(2,1)S(1)}, u32[]{:S(2)}, u32[]{:S(2)}) %collective-permute-start) | collective-permute-done | bytes 524320 | tf_op jit(solution)/shard_map/while/body/eval_jaxpr/ppermute | solution.py:16
  500.7 21.3 %collective-permute-done = bf16[2,128,8,128]{3,1,2,0:T(8,128)(2,1)S(1)} collective-permute-done((bf16[2,128,8,128]{3,1,2,0:T(8,128)(2,1)S(1)}, bf16[2,128,8,128]{3,1,2,0:T(8,128)(2,1)S(1)}, u32[]{:S(2)}, u32[]{:S(2)}) %collective-permute-start) | collective-permute-done | bytes 524320 | tf_op jit(solution)/shard_map/while/body/eval_jaxpr/ppermute | solution.py:16
  531.0 19.5 %collective-permute-done = bf16[2,128,8,128]{3,1,2,0:T(8,128)(2,1)S(1)} collective-permute-done((bf16[2,128,8,128]{3,1,2,0:T(8,128)(2,1)S(1)}, bf16[2,128,8,128]{3,1,2,0:T(8,128)(2,1)S(1)}, u32[]{:S(2)}, u32[]{:S(2)}) %collective-permute-start) | collective-permute-done | bytes 524320 | tf_op jit(solution)/shard_map/while/body/eval_jaxpr/ppermute | solution.py:16
  559.5 21.3 %collective-permute-done = bf16[2,128,8,128]{3,1,2,0:T(8,128)(2,1)S(1)} collective-permute-done((bf16[2,128,8,128]{3,1,2,0:T(8,128)(2,1)S(1)}, bf16[2,128,8,128]{3,1,2,0:T(8,128)(2,1)S(1)}, u32[]{:S(2)}, u32[]{:S(2)}) %collective-permute-start) | collective-permute-done | bytes 524320 | tf_op jit(solution)/shard_map/while/body/eval_jaxpr/ppermute | solution.py:16
  589.7 19.5 %collective-permute-done = bf16[2,128,8,128]{3,1,2,0:T(8,128)(2,1)S(1)} collective-permute-done((bf16[2,128,8,128]{3,1,2,0:T(8,128)(2,1)S(1)}, bf16[2,128,8,128]{3,1,2,0:T(8,128)(2,1)S(1)}, u32[]{:S(2)}, u32[]{:S(2)}) %collective-permute-start) | collective-permute-done | bytes 524320 | tf_op jit(solution)/shard_map/while/body/eval_jaxpr/ppermute | solution.py:16
  618.2 21.3 %collective-permute-done = bf16[2,128,8,128]{3,1,2,0:T(8,128)(2,1)S(1)} collective-permute-done((bf16[2,128,8,128]{3,1,2,0:T(8,128)(2,1)S(1)}, bf16[2,128,8,128]{3,1,2,0:T(8,128)(2,1)S(1)}, u32[]{:S(2)}, u32[]{:S(2)}) %collective-permute-start) | collective-permute-done | bytes 524320 | tf_op jit(solution)/shard_map/while/body/eval_jaxpr/ppermute | solution.py:16
  648.5 19.5 %collective-permute-done = bf16[2,128,8,128]{3,1,2,0:T(8,128)(2,1)S(1)} collective-permute-done((bf16[2,128,8,128]{3,1,2,0:T(8,128)(2,1)S(1)}, bf16[2,128,8,128]{3,1,2,0:T(8,128)(2,1)S(1)}, u32[]{:S(2)}, u32[]{:S(2)}) %collective-permute-start) | collective-permute-done | bytes 524320 | tf_op jit(solution)/shard_map/while/body/eval_jaxpr/ppermute | solution.py:16
  676.9 21.3 %collective-permute-done = bf16[2,128,8,128]{3,1,2,0:T(8,128)(2,1)S(1)} collective-permute-done((bf16[2,128,8,128]{3,1,2,0:T(8,128)(2,1)S(1)}, bf16[2,128,8,128]{3,1,2,0:T(8,128)(2,1)S(1)}, u32[]{:S(2)}, u32[]{:S(2)}) %collective-permute-start) | collective-permute-done | bytes 524320 | tf_op jit(solution)/shard_map/while/body/eval_jaxpr/ppermute | solution.py:16
  707.2 19.5 %collective-permute-done = bf16[2,128,8,128]{3,1,2,0:T(8,128)(2,1)S(1)} collective-permute-done((bf16[2,128,8,128]{3,1,2,0:T(8,128)(2,1)S(1)}, bf16[2,128,8,128]{3,1,2,0:T(8,128)(2,1)S(1)}, u32[]{:S(2)}, u32[]{:S(2)}) %collective-permute-start) | collective-permute-done | bytes 524320 | tf_op jit(solution)/shard_map/while/body/eval_jaxpr/ppermute | solution.py:16
  735.7 21.3 %collective-permute-done = bf16[2,128,8,128]{3,1,2,0:T(8,128)(2,1)S(1)} collective-permute-done((bf16[2,128,8,128]{3,1,2,0:T(8,128)(2,1)S(1)}, bf16[2,128,8,128]{3,1,2,0:T(8,128)(2,1)S(1)}, u32[]{:S(2)}, u32[]{:S(2)}) %collective-permute-start) | collective-permute-done | bytes 524320 | tf_op jit(solution)/shard_map/while/body/eval_jaxpr/ppermute | solution.py:16
  765.9 19.5 %collective-permute-done = bf16[2,128,8,128]{3,1,2,0:T(8,128)(2,1)S(1)} collective-permute-done((bf16[2,128,8,128]{3,1,2,0:T(8,128)(2,1)S(1)}, bf16[2,128,8,128]{3,1,2,0:T(8,128)(2,1)S(1)}, u32[]{:S(2)}, u32[]{:S(2)}) %collective-permute-start) | collective-permute-done | bytes 524320 | tf_op jit(solution)/shard_map/while/body/eval_jaxpr/ppermute | solution.py:16
  796.2 15.8 %all-reduce.2.cloned.1.call-done = f32[128,2048]{1,0:T(8,128)} async-done(((f32[128,2048]{1,0:T(8,128)}), f32[128,2048]{1,0:T(8,128)}) %all-reduce.2.cloned.1.call-update) | async-done | bytes 1048592 | tf_op jit(solution)/shard_map/psum | solution.py:183
  814.5 6.0 gather_fusion.1
  825.4 110.3 %all_to_all.22 = bf16[16,72,2048]{2,1,0:T(8,128)(2,1)S(1)} all-to-all(bf16[16,72,2048]{2,1,0:T(8,128)(2,1)} %broadcast_select_fusion.1), channel_id=1, replica_groups=mesh['seq'=16,'tp'=2] {'seq'}, dimensions={0} | all-to-all | bytes 9437184 | tf_op jit(solution)/shard_map/all_to_all | solution.py:215
  935.7 7.3 fusion.14
  943.0 5.9 convert_bitcast_fusion
  973.4 5.4 collective-permute-done.7
  984.2 5.4 collective-permute-done.9
  1026.1 34.7 %all-to-all-start.2 = ((bf16[16,72,1024]{2,1,0:T(8,128)(2,1)}), bf16[16,72,1024]{2,1,0:T(8,128)(2,1)S(1)}, u32[]{:S(2)}, u32[]{:S(2)}) async-start(bf16[16,72,1024]{2,1,0:T(8,128)(2,1)} %bitcast.101), calls=%async_computation.3 | async-start | bytes 4718592 | tf_op jit(solution)/shard_map/all_to_all | solution.py:237
  1061.7 32.9 %all-to-all-done.2 = bf16[16,72,1024]{2,1,0:T(8,128)(2,1)S(1)} async-done(((bf16[16,72,1024]{2,1,0:T(8,128)(2,1)}), bf16[16,72,1024]{2,1,0:T(8,128)(2,1)S(1)}, u32[]{:S(2)}, u32[]{:S(2)}) %all-to-all-start.2) | async-done | bytes 2359328 | tf_op jit(solution)/shard_map/all_to_all | solution.py:237
  (484 shorter events, 256.8 us)
Async XLA Ops:
  6.5 277.5 %all-gather.3.cloned.1.call-start = ((), (), s32[]{:S(2)}) async-start(), calls=%async_computation.4 | async-start | bytes 13369344 | tf_op jit(solution)/shard_map/all_gather | solution.py:121
  35.2 790.2 %all-to-all-start = ((bf16[16,128,1536]{2,1,0:T(8,128)(2,1)}), bf16[16,128,1536]{2,1,0:T(8,128)(2,1)}, u32[]{:S(2)}, u32[]{:S(2)}) async-start(bf16[16,128,1536]{2,1,0:T(8,128)(2,1)} %broadcast_select_fusion), calls=%async_computation | async-start | bytes 12582912 | tf_op jit(solution)/shard_map/all_to_all | solution.py:212
  42.5 745.1 %all-gather.5.cloned.1.call-start = ((), (), s32[]{:S(2)}) async-start(), calls=%async_computation.5 | async-start | bytes 4456448 | tf_op jit(solution)/shard_map/all_gather | solution.py:180
  43.3 768.7 %all-reduce.2.cloned.1.call-start = ((), (), s32[]{:S(2)}) async-start(), calls=%async_computation.6 | async-start | bytes 2097152 | tf_op jit(solution)/shard_map/psum | solution.py:183
  293.5 30.4 %collective-permute-start.1 = (bf16[2,128,8,128]{3,1,2,0:T(8,128)(2,1)S(1)}, bf16[2,128,8,128]{3,1,2,0:T(8,128)(2,1)S(1)}, u32[]{:S(2)}, u32[]{:S(2)}) collective-permute-start(bf16[2,128,8,128]{3,1,2,0:T(8,128)(2,1)S(1)} %get-tuple-element.428), channel_id=1, source_target_pairs={{2,0},{4,2},{6,4},{8,6},{10,8},{12,10},{14,12},{16,14},{18,16},{20... | collective-permute-start | bytes 1572872 | tf_op jit(solution)/shard_map/while/body/eval_jaxpr/ppermute | solution.py:16
  296.2 27.7 %collective-permute-start = (bf16[2,128,8,128]{3,1,2,0:T(8,128)(2,1)S(1)}, bf16[2,128,8,128]{3,1,2,0:T(8,128)(2,1)S(1)}, u32[]{:S(2)}, u32[]{:S(2)}) collective-permute-start(bf16[2,128,8,128]{3,1,2,0:T(8,128)(2,1)S(1)} %get-tuple-element.427), channel_id=1, source_target_pairs={{0,2},{2,4},{4,6},{6,8},{8,10},{10,12},{12,14},{14,16},{16,18},{18... | collective-permute-start | bytes 1572872 | tf_op jit(solution)/shard_map/while/body/eval_jaxpr/ppermute | solution.py:16
  325.8 27.9 %collective-permute-start.1 = (bf16[2,128,8,128]{3,1,2,0:T(8,128)(2,1)S(1)}, bf16[2,128,8,128]{3,1,2,0:T(8,128)(2,1)S(1)}, u32[]{:S(2)}, u32[]{:S(2)}) collective-permute-start(bf16[2,128,8,128]{3,1,2,0:T(8,128)(2,1)S(1)} %get-tuple-element.428), channel_id=1, source_target_pairs={{2,0},{4,2},{6,4},{8,6},{10,8},{12,10},{14,12},{16,14},{18,16},{20... | collective-permute-start | bytes 1572872 | tf_op jit(solution)/shard_map/while/body/eval_jaxpr/ppermute | solution.py:16
  327.7 25.9 %collective-permute-start = (bf16[2,128,8,128]{3,1,2,0:T(8,128)(2,1)S(1)}, bf16[2,128,8,128]{3,1,2,0:T(8,128)(2,1)S(1)}, u32[]{:S(2)}, u32[]{:S(2)}) collective-permute-start(bf16[2,128,8,128]{3,1,2,0:T(8,128)(2,1)S(1)} %get-tuple-element.427), channel_id=1, source_target_pairs={{0,2},{2,4},{4,6},{6,8},{8,10},{10,12},{12,14},{14,16},{16,18},{18... | collective-permute-start | bytes 1572872 | tf_op jit(solution)/shard_map/while/body/eval_jaxpr/ppermute | solution.py:16
  355.5 48.5 %collective-permute-start.1 = (bf16[2,128,8,128]{3,1,2,0:T(8,128)(2,1)S(1)}, bf16[2,128,8,128]{3,1,2,0:T(8,128)(2,1)S(1)}, u32[]{:S(2)}, u32[]{:S(2)}) collective-permute-start(bf16[2,128,8,128]{3,1,2,0:T(8,128)(2,1)S(1)} %get-tuple-element.428), channel_id=1, source_target_pairs={{2,0},{4,2},{6,4},{8,6},{10,8},{12,10},{14,12},{16,14},{18,16},{20... | collective-permute-start | bytes 1572872 | tf_op jit(solution)/shard_map/while/body/eval_jaxpr/ppermute | solution.py:16
  359.3 44.6 %collective-permute-start = (bf16[2,128,8,128]{3,1,2,0:T(8,128)(2,1)S(1)}, bf16[2,128,8,128]{3,1,2,0:T(8,128)(2,1)S(1)}, u32[]{:S(2)}, u32[]{:S(2)}) collective-permute-start(bf16[2,128,8,128]{3,1,2,0:T(8,128)(2,1)S(1)} %get-tuple-element.427), channel_id=1, source_target_pairs={{0,2},{2,4},{4,6},{6,8},{8,10},{10,12},{12,14},{14,16},{16,18},{18... | collective-permute-start | bytes 1572872 | tf_op jit(solution)/shard_map/while/body/eval_jaxpr/ppermute | solution.py:16
  405.8 28.8 %collective-permute-start.1 = (bf16[2,128,8,128]{3,1,2,0:T(8,128)(2,1)S(1)}, bf16[2,128,8,128]{3,1,2,0:T(8,128)(2,1)S(1)}, u32[]{:S(2)}, u32[]{:S(2)}) collective-permute-start(bf16[2,128,8,128]{3,1,2,0:T(8,128)(2,1)S(1)} %get-tuple-element.428), channel_id=1, source_target_pairs={{2,0},{4,2},{6,4},{8,6},{10,8},{12,10},{14,12},{16,14},{18,16},{20... | collective-permute-start | bytes 1572872 | tf_op jit(solution)/shard_map/while/body/eval_jaxpr/ppermute | solution.py:16
  407.7 26.8 %collective-permute-start = (bf16[2,128,8,128]{3,1,2,0:T(8,128)(2,1)S(1)}, bf16[2,128,8,128]{3,1,2,0:T(8,128)(2,1)S(1)}, u32[]{:S(2)}, u32[]{:S(2)}) collective-permute-start(bf16[2,128,8,128]{3,1,2,0:T(8,128)(2,1)S(1)} %get-tuple-element.427), channel_id=1, source_target_pairs={{0,2},{2,4},{4,6},{6,8},{8,10},{10,12},{12,14},{14,16},{16,18},{18... | collective-permute-start | bytes 1572872 | tf_op jit(solution)/shard_map/while/body/eval_jaxpr/ppermute | solution.py:16
  436.4 26.9 %collective-permute-start.1 = (bf16[2,128,8,128]{3,1,2,0:T(8,128)(2,1)S(1)}, bf16[2,128,8,128]{3,1,2,0:T(8,128)(2,1)S(1)}, u32[]{:S(2)}, u32[]{:S(2)}) collective-permute-start(bf16[2,128,8,128]{3,1,2,0:T(8,128)(2,1)S(1)} %get-tuple-element.428), channel_id=1, source_target_pairs={{2,0},{4,2},{6,4},{8,6},{10,8},{12,10},{14,12},{16,14},{18,16},{20... | collective-permute-start | bytes 1572872 | tf_op jit(solution)/shard_map/while/body/eval_jaxpr/ppermute | solution.py:16
  465.2 26.6 %collective-permute-start.1 = (bf16[2,128,8,128]{3,1,2,0:T(8,128)(2,1)S(1)}, bf16[2,128,8,128]{3,1,2,0:T(8,128)(2,1)S(1)}, u32[]{:S(2)}, u32[]{:S(2)}) collective-permute-start(bf16[2,128,8,128]{3,1,2,0:T(8,128)(2,1)S(1)} %get-tuple-element.428), channel_id=1, source_target_pairs={{2,0},{4,2},{6,4},{8,6},{10,8},{12,10},{14,12},{16,14},{18,16},{20... | collective-permute-start | bytes 1572872 | tf_op jit(solution)/shard_map/while/body/eval_jaxpr/ppermute | solution.py:16
  493.6 28.4 %collective-permute-start.1 = (bf16[2,128,8,128]{3,1,2,0:T(8,128)(2,1)S(1)}, bf16[2,128,8,128]{3,1,2,0:T(8,128)(2,1)S(1)}, u32[]{:S(2)}, u32[]{:S(2)}) collective-permute-start(bf16[2,128,8,128]{3,1,2,0:T(8,128)(2,1)S(1)} %get-tuple-element.428), channel_id=1, source_target_pairs={{2,0},{4,2},{6,4},{8,6},{10,8},{12,10},{14,12},{16,14},{18,16},{20... | collective-permute-start | bytes 1572872 | tf_op jit(solution)/shard_map/while/body/eval_jaxpr/ppermute | solution.py:16
  495.6 26.4 %collective-permute-start = (bf16[2,128,8,128]{3,1,2,0:T(8,128)(2,1)S(1)}, bf16[2,128,8,128]{3,1,2,0:T(8,128)(2,1)S(1)}, u32[]{:S(2)}, u32[]{:S(2)}) collective-permute-start(bf16[2,128,8,128]{3,1,2,0:T(8,128)(2,1)S(1)} %get-tuple-element.427), channel_id=1, source_target_pairs={{0,2},{2,4},{4,6},{6,8},{8,10},{10,12},{12,14},{14,16},{16,18},{18... | collective-permute-start | bytes 1572872 | tf_op jit(solution)/shard_map/while/body/eval_jaxpr/ppermute | solution.py:16
  523.9 26.6 %collective-permute-start.1 = (bf16[2,128,8,128]{3,1,2,0:T(8,128)(2,1)S(1)}, bf16[2,128,8,128]{3,1,2,0:T(8,128)(2,1)S(1)}, u32[]{:S(2)}, u32[]{:S(2)}) collective-permute-start(bf16[2,128,8,128]{3,1,2,0:T(8,128)(2,1)S(1)} %get-tuple-element.428), channel_id=1, source_target_pairs={{2,0},{4,2},{6,4},{8,6},{10,8},{12,10},{14,12},{16,14},{18,16},{20... | collective-permute-start | bytes 1572872 | tf_op jit(solution)/shard_map/while/body/eval_jaxpr/ppermute | solution.py:16
  552.4 28.4 %collective-permute-start.1 = (bf16[2,128,8,128]{3,1,2,0:T(8,128)(2,1)S(1)}, bf16[2,128,8,128]{3,1,2,0:T(8,128)(2,1)S(1)}, u32[]{:S(2)}, u32[]{:S(2)}) collective-permute-start(bf16[2,128,8,128]{3,1,2,0:T(8,128)(2,1)S(1)} %get-tuple-element.428), channel_id=1, source_target_pairs={{2,0},{4,2},{6,4},{8,6},{10,8},{12,10},{14,12},{16,14},{18,16},{20... | collective-permute-start | bytes 1572872 | tf_op jit(solution)/shard_map/while/body/eval_jaxpr/ppermute | solution.py:16
  554.3 26.4 %collective-permute-start = (bf16[2,128,8,128]{3,1,2,0:T(8,128)(2,1)S(1)}, bf16[2,128,8,128]{3,1,2,0:T(8,128)(2,1)S(1)}, u32[]{:S(2)}, u32[]{:S(2)}) collective-permute-start(bf16[2,128,8,128]{3,1,2,0:T(8,128)(2,1)S(1)} %get-tuple-element.427), channel_id=1, source_target_pairs={{0,2},{2,4},{4,6},{6,8},{8,10},{10,12},{12,14},{14,16},{16,18},{18... | collective-permute-start | bytes 1572872 | tf_op jit(solution)/shard_map/while/body/eval_jaxpr/ppermute | solution.py:16
  582.6 26.6 %collective-permute-start.1 = (bf16[2,128,8,128]{3,1,2,0:T(8,128)(2,1)S(1)}, bf16[2,128,8,128]{3,1,2,0:T(8,128)(2,1)S(1)}, u32[]{:S(2)}, u32[]{:S(2)}) collective-permute-start(bf16[2,128,8,128]{3,1,2,0:T(8,128)(2,1)S(1)} %get-tuple-element.428), channel_id=1, source_target_pairs={{2,0},{4,2},{6,4},{8,6},{10,8},{12,10},{14,12},{16,14},{18,16},{20... | collective-permute-start | bytes 1572872 | tf_op jit(solution)/shard_map/while/body/eval_jaxpr/ppermute | solution.py:16
  611.1 28.4 %collective-permute-start.1 = (bf16[2,128,8,128]{3,1,2,0:T(8,128)(2,1)S(1)}, bf16[2,128,8,128]{3,1,2,0:T(8,128)(2,1)S(1)}, u32[]{:S(2)}, u32[]{:S(2)}) collective-permute-start(bf16[2,128,8,128]{3,1,2,0:T(8,128)(2,1)S(1)} %get-tuple-element.428), channel_id=1, source_target_pairs={{2,0},{4,2},{6,4},{8,6},{10,8},{12,10},{14,12},{16,14},{18,16},{20... | collective-permute-start | bytes 1572872 | tf_op jit(solution)/shard_map/while/body/eval_jaxpr/ppermute | solution.py:16
  613.1 26.4 %collective-permute-start = (bf16[2,128,8,128]{3,1,2,0:T(8,128)(2,1)S(1)}, bf16[2,128,8,128]{3,1,2,0:T(8,128)(2,1)S(1)}, u32[]{:S(2)}, u32[]{:S(2)}) collective-permute-start(bf16[2,128,8,128]{3,1,2,0:T(8,128)(2,1)S(1)} %get-tuple-element.427), channel_id=1, source_target_pairs={{0,2},{2,4},{4,6},{6,8},{8,10},{10,12},{12,14},{14,16},{16,18},{18... | collective-permute-start | bytes 1572872 | tf_op jit(solution)/shard_map/while/body/eval_jaxpr/ppermute | solution.py:16
  641.4 26.6 %collective-permute-start.1 = (bf16[2,128,8,128]{3,1,2,0:T(8,128)(2,1)S(1)}, bf16[2,128,8,128]{3,1,2,0:T(8,128)(2,1)S(1)}, u32[]{:S(2)}, u32[]{:S(2)}) collective-permute-start(bf16[2,128,8,128]{3,1,2,0:T(8,128)(2,1)S(1)} %get-tuple-element.428), channel_id=1, source_target_pairs={{2,0},{4,2},{6,4},{8,6},{10,8},{12,10},{14,12},{16,14},{18,16},{20... | collective-permute-start | bytes 1572872 | tf_op jit(solution)/shard_map/while/body/eval_jaxpr/ppermute | solution.py:16
  669.9 28.4 %collective-permute-start.1 = (bf16[2,128,8,128]{3,1,2,0:T(8,128)(2,1)S(1)}, bf16[2,128,8,128]{3,1,2,0:T(8,128)(2,1)S(1)}, u32[]{:S(2)}, u32[]{:S(2)}) collective-permute-start(bf16[2,128,8,128]{3,1,2,0:T(8,128)(2,1)S(1)} %get-tuple-element.428), channel_id=1, source_target_pairs={{2,0},{4,2},{6,4},{8,6},{10,8},{12,10},{14,12},{16,14},{18,16},{20... | collective-permute-start | bytes 1572872 | tf_op jit(solution)/shard_map/while/body/eval_jaxpr/ppermute | solution.py:16
  671.8 26.4 %collective-permute-start = (bf16[2,128,8,128]{3,1,2,0:T(8,128)(2,1)S(1)}, bf16[2,128,8,128]{3,1,2,0:T(8,128)(2,1)S(1)}, u32[]{:S(2)}, u32[]{:S(2)}) collective-permute-start(bf16[2,128,8,128]{3,1,2,0:T(8,128)(2,1)S(1)} %get-tuple-element.427), channel_id=1, source_target_pairs={{0,2},{2,4},{4,6},{6,8},{8,10},{10,12},{12,14},{14,16},{16,18},{18... | collective-permute-start | bytes 1572872 | tf_op jit(solution)/shard_map/while/body/eval_jaxpr/ppermute | solution.py:16
  700.1 26.6 %collective-permute-start.1 = (bf16[2,128,8,128]{3,1,2,0:T(8,128)(2,1)S(1)}, bf16[2,128,8,128]{3,1,2,0:T(8,128)(2,1)S(1)}, u32[]{:S(2)}, u32[]{:S(2)}) collective-permute-start(bf16[2,128,8,128]{3,1,2,0:T(8,128)(2,1)S(1)} %get-tuple-element.428), channel_id=1, source_target_pairs={{2,0},{4,2},{6,4},{8,6},{10,8},{12,10},{14,12},{16,14},{18,16},{20... | collective-permute-start | bytes 1572872 | tf_op jit(solution)/shard_map/while/body/eval_jaxpr/ppermute | solution.py:16
  728.6 28.4 %collective-permute-start.1 = (bf16[2,128,8,128]{3,1,2,0:T(8,128)(2,1)S(1)}, bf16[2,128,8,128]{3,1,2,0:T(8,128)(2,1)S(1)}, u32[]{:S(2)}, u32[]{:S(2)}) collective-permute-start(bf16[2,128,8,128]{3,1,2,0:T(8,128)(2,1)S(1)} %get-tuple-element.428), channel_id=1, source_target_pairs={{2,0},{4,2},{6,4},{8,6},{10,8},{12,10},{14,12},{16,14},{18,16},{20... | collective-permute-start | bytes 1572872 | tf_op jit(solution)/shard_map/while/body/eval_jaxpr/ppermute | solution.py:16
  730.5 26.4 %collective-permute-start = (bf16[2,128,8,128]{3,1,2,0:T(8,128)(2,1)S(1)}, bf16[2,128,8,128]{3,1,2,0:T(8,128)(2,1)S(1)}, u32[]{:S(2)}, u32[]{:S(2)}) collective-permute-start(bf16[2,128,8,128]{3,1,2,0:T(8,128)(2,1)S(1)} %get-tuple-element.427), channel_id=1, source_target_pairs={{0,2},{2,4},{4,6},{6,8},{8,10},{10,12},{12,14},{14,16},{16,18},{18... | collective-permute-start | bytes 1572872 | tf_op jit(solution)/shard_map/while/body/eval_jaxpr/ppermute | solution.py:16
  758.8 26.6 %collective-permute-start.1 = (bf16[2,128,8,128]{3,1,2,0:T(8,128)(2,1)S(1)}, bf16[2,128,8,128]{3,1,2,0:T(8,128)(2,1)S(1)}, u32[]{:S(2)}, u32[]{:S(2)}) collective-permute-start(bf16[2,128,8,128]{3,1,2,0:T(8,128)(2,1)S(1)} %get-tuple-element.428), channel_id=1, source_target_pairs={{2,0},{4,2},{6,4},{8,6},{10,8},{12,10},{14,12},{16,14},{18,16},{20... | collective-permute-start | bytes 1572872 | tf_op jit(solution)/shard_map/while/body/eval_jaxpr/ppermute | solution.py:16
  791.6 234.6 %reduce-scatter.2.cloned.1.call-start = ((), (), s32[]{:S(2)}) async-start(), calls=%async_computation.7 | async-start | bytes 7077888 | tf_op jit(solution)/shard_map/reduce_scatter | solution.py:234
  1022.1 38.8 %collective-permute-start.16 = (bf16[128,16]{0,1:T(8,128)(2,1)S(1)}, bf16[128,16]{0,1:T(8,128)(2,1)S(1)}, u32[]{:S(2)}, u32[]{:S(2)}) collective-permute-start(bf16[128,16]{0,1:T(8,128)(2,1)S(1)} %collective-permute-done.15), channel_id=1, source_target_pairs={{0,2},{2,4},{4,6},{6,8},{8,10},{10,12},{12,14},{14,16},{16,18},{18... | collective-permute-start | bytes 12296 | tf_op jit(solution)/shard_map/ppermute | solution.py:126
  1026.1 68.5 %all-to-all-start.2 = ((bf16[16,72,1024]{2,1,0:T(8,128)(2,1)}), bf16[16,72,1024]{2,1,0:T(8,128)(2,1)S(1)}, u32[]{:S(2)}, u32[]{:S(2)}) async-start(bf16[16,72,1024]{2,1,0:T(8,128)(2,1)} %bitcast.101), calls=%async_computation.3 | async-start | bytes 4718592 | tf_op jit(solution)/shard_map/all_to_all | solution.py:237
  (33 other events, 563.7 us)
Sparse Core Ops, SparseCore 0:
  10.9 273.0 all-gather.2
  286.7 137.9 all-gather.4
  791.7 20.2 all-reduce.1
  949.1 12.8 reduce-scatter.1
